TPU v7x, 512 devices: a whole 4x8x8 slice. The times are simulated.
512 devices in a mesh: context: 32 (over y, x), tensor: 16 (over z, core).
Axes of the slice: x: 4, y: 8, z: 8, core: 2. Of those that a mesh axis runs over, the one named last changes fastest.
Arguments:
- queries: bfloat16 [1, 16384, 4096], P(None, 'context', 'tensor'), may hold values from -6 to 6
- keys: bfloat16 [1, 16384, 4096], P(None, 'context', 'tensor'), may hold values from -0.546875 to 0.546875
- spike_counts: int32 [1, 16384, 4096], P(None, 'context', 'tensor'), may hold values from -4 to 4
- spike_scale: float32 [4096], P('tensor'), may hold values from 0.5 to 2
- log_decay: float32 [1, 32, 16384], P(None, 'tensor', 'context'), may hold values from -3 to 0, as said below
- norm_gain: float32 [4096], P('tensor'), may hold values from 0.5 to 1.5
- out_weight: bfloat16 [4096, 8192], P('context', 'tensor'), may hold values from -0.09375 to 0.09375
- residual_in: bfloat16 [1, 16384, 8192], P(None, 'context', 'tensor'), may hold values from -6 to 6
Outputs:
- residual_out: bfloat16 [1, 16384, 8192], P(None, 'context', 'tensor')
Inputs may be any that keep to these rules, and one draw needn't show every extreme that they name: log_decay is negative.
All inputs are finite; a program needn't handle non-finite values.
Results may differ from a plain program's by a relative error of at most 0.0095.
Values may be sent and summed in bfloat16 or wider, within the bound.
A program may use at most 64 MiB of HBM per device.

v0:
```python
import jax
import jax.numpy as jnp
from jax import lax
from jax.sharding import PartitionSpec as P

epsilon = 1e-06


def prefix_2(value, axis, combine, identity):
    size, position = (lax.axis_size(axis), lax.axis_index(axis))
    everything = jax.tree.map(
        lambda part, kind: lax.all_gather(part.astype(kind), axis),
        value,
        (jnp.bfloat16, jnp.bfloat16),
    )
    start = jax.tree.map(
        lambda part, zero: jnp.broadcast_to(jnp.asarray(zero, part.dtype), part.shape),
        value,
        identity,
    )

    def lap(k, before):
        reached = k < position
        new = combine(
            before, jax.tree.map(lambda part, own: part[k].astype(own.dtype), everything, value)
        )
        return jax.tree.map(lambda a, b: jnp.where(reached, a, b), new, before)

    return lax.fori_loop(0, size, lap, start)


def combine(earlier, later):
    return (earlier[0] * later[0], later[0][..., None, None] * earlier[1] + later[1])


def local(queries, keys, spike_counts, spike_scale, log_decay, norm_gain, out_weight, residual_in):
    requests, block, width_here = queries.shape
    heads = log_decay.shape[1]
    head_size = width_here // heads
    values = (spike_counts.astype(jnp.float32) * spike_scale).astype(jnp.bfloat16)

    def split_heads(array):
        return array.reshape(requests, block, heads, head_size).transpose(0, 2, 1, 3)

    query_h = split_heads(queries)
    key_h = split_heads(keys)
    value_h = split_heads(values)
    cumulative = jnp.cumsum(log_decay, axis=2)
    vocabulary_identifiers = jnp.arange(block)
    causal = vocabulary_identifiers[:, None] >= vocabulary_identifiers[None, :]
    gaps = cumulative[..., :, None] - cumulative[..., None, :]
    decay_mat = jnp.exp(jnp.where(causal, gaps, -1e30))
    scores = jnp.einsum("rhtd,rhsd->rhts", query_h, key_h, preferred_element_type=jnp.float32)
    weights = (scores * decay_mat).astype(jnp.bfloat16)
    intra = jnp.einsum("rhts,rhsd->rhtd", weights, value_h, preferred_element_type=jnp.float32)
    to_end = jnp.exp(cumulative[..., -1:] - cumulative)
    weighted_keys = (key_h.astype(jnp.float32) * to_end[..., None]).astype(jnp.bfloat16)
    own_state = jnp.einsum(
        "rhsd,rhse->rhde", weighted_keys, value_h, preferred_element_type=jnp.float32
    )
    span_decay = jnp.exp(cumulative[..., -1])
    prefix = prefix_2(
        (span_decay, own_state),
        "context",
        combine,
        (jnp.ones_like(span_decay), jnp.zeros_like(own_state)),
    )
    incoming = prefix[1]
    carried = jnp.exp(cumulative)[..., None] * jnp.einsum(
        "rhtd,rhde->rhte", query_h.astype(jnp.float32), incoming, precision=lax.Precision.HIGHEST
    )
    mixed = intra + carried
    scale = lax.rsqrt(jnp.mean(mixed * mixed, axis=-1, keepdims=True) + epsilon)
    normed = (mixed * scale * norm_gain.reshape(1, heads, 1, head_size)).astype(jnp.bfloat16)
    normed = normed.transpose(0, 2, 1, 3).reshape(requests * block, width_here)
    all_heads = lax.all_gather(normed, "tensor", axis=1, tiled=True)
    projected = jnp.dot(
        all_heads,
        lax.all_gather(out_weight, "context", axis=0, tiled=True),
        preferred_element_type=jnp.float32,
    )
    projected = projected.reshape(requests, block, out_weight.shape[1])
    return (residual_in.astype(jnp.float32) + projected).astype(jnp.bfloat16)


def solution(mesh):
    in_specs = (
        P(None, "context", "tensor"),
        P(None, "context", "tensor"),
        P(None, "context", "tensor"),
        P("tensor"),
        P(None, "tensor", "context"),
        P("tensor"),
        P("context", "tensor"),
        P(None, "context", "tensor"),
    )
    out_specs = P(None, "context", "tensor")
    return jax.shard_map(local, mesh=mesh, in_specs=in_specs, out_specs=out_specs, check_vma=False)
```

profile of v0, /device:TPU:1, one launch (start us, length us, event | category | flops | bytes accessed | tf_op | source)
XLA Modules:
  0.0 247.4 jit_solution(11480079209673487597)
XLA Ops:
  6.5 0.7 reshape.238
  7.3 0.6 reduce-window.6
  7.9 0.2 slice_reduce_fusion
  8.1 0.2 reduce-window.9
  8.4 1.1 copy.44
  9.5 1.1 multiply_convert_fusion.3
  10.6 0.2 exponential_convert_fusion
  10.9 0.9 convolution_convert_fusion
  11.9 0.7 all-gather.8.cloned.1.call-update
  12.7 31.4 %all-gather = bf16[32,2,1]{2,1,0:T(2,128)(2,1)S(1)} all-gather(bf16[1,2,1]{2,1,0:T(2,128)(2,1)S(1)} %get-tuple-element.154), channel_id=2, replica_groups=mesh['context'=32,'tensor'=16] {'context'}, dimensions={0}, use_global_device_ids=true | all-gather | bytes 132 | tf_op jit(solution)/shard_map/all_gather | solution.py:12
  44.3 52.7 %all-gather.10.cloned.1.call-done = bf16[64,128,128]{2,1,0:T(8,128)(2,1)} async-done(((bf16[2,128,128]{2,1,0:T(8,128)(2,1)}), bf16[64,128,128]{2,1,0:T(8,128)(2,1)}) %all-gather.10.cloned.1.call-update) | async-done | bytes 2097168 | tf_op jit(solution)/shard_map/all_gather | solution.py:12
  97.0 36.8 %while.14 = (s32[]{:T(128)}, f32[1,2,128,128]{3,2,1,0:T(8,128)S(1)}, s32[]{:T(128)}, bf16[32,1,2]{0,2,1:T(2,128)(2,1)S(1)}, bf16[32,1,2,128,128]{4,3,2,1,0:T(8,128)(2,1)}, /*index=5*/s32[]{:T(128)}, s32[]{:T(128)}) while((s32[]{:T(128)}, f32[1,2,128,128]{3,2,1,0:T(8,128)S(1)}, s32[]{:T(128)}, bf16[32,1,2]{0,2,1:T(2,128)(2,1)S(1)}, ...), condition=%wide.region_3.4_spmd.clone, body=%wide.region_2.3_spmd.clone.sunk | while | flops 163846 | bytes 327829 | solution.py:29
  97.1 0.1 copy.53
  97.2 0.9 fusion.25
  98.2 0.1 copy.53
  98.3 0.9 fusion.25
  99.4 0.1 copy.53
  99.5 0.9 fusion.25
  100.5 0.1 copy.53
  100.6 0.9 fusion.25
  101.7 0.1 copy.53
  101.8 0.9 fusion.25
  102.8 0.1 copy.53
  102.9 0.9 fusion.25
  104.1 0.9 fusion.25
  105.2 0.9 fusion.25
  106.4 0.9 fusion.25
  107.5 0.9 fusion.25
  108.7 0.9 fusion.25
  109.8 0.9 fusion.25
  110.8 0.1 copy.53
  111.0 0.9 fusion.25
  112.1 0.9 fusion.25
  113.3 0.9 fusion.25
  114.3 0.1 copy.53
  114.4 0.9 fusion.25
  115.6 0.9 fusion.25
  116.6 0.1 copy.53
  116.7 0.9 fusion.25
  117.9 0.9 fusion.25
  119.0 0.9 fusion.25
  120.2 0.9 fusion.25
  121.3 0.9 fusion.25
  122.5 0.9 fusion.25
  123.6 0.9 fusion.25
  124.8 0.9 fusion.25
  125.9 0.9 fusion.25
  126.9 0.1 copy.53
  127.1 0.9 fusion.25
  128.2 0.9 fusion.25
  129.2 0.1 copy.53
  129.4 0.9 fusion.25
  130.4 0.1 copy.53
  130.5 0.9 fusion.25
  131.5 0.1 copy.53
  131.7 0.9 fusion.25
  132.7 0.1 copy.53
  132.8 0.9 fusion.25
  133.7 0.4 convolution_multiply_fusion
  134.2 1.0 multiply_reduce_fusion
  135.3 0.8 multiply_convert_fusion.1
  136.1 49.7 %all-gather.8.cloned.1.call-done = bf16[4096,512]{1,0:T(8,128)(2,1)} async-done(((bf16[128,512]{1,0:T(8,128)(2,1)}), bf16[4096,512]{1,0:T(8,128)(2,1)}) %all-gather.8.cloned.1.call-update) | async-done | bytes 4194320 | tf_op jit(solution)/shard_map/all_gather | solution.py:79
  185.8 48.4 %all-gather.6.cloned.1.call-done = bf16[512,4096]{0,1:T(8,128)(2,1)} async-done(((bf16[512,256]{0,1:T(8,128)(2,1)}), bf16[512,4096]{0,1:T(8,128)(2,1)}) %all-gather.6.cloned.1.call-update) | async-done | bytes 4194320 | tf_op jit(solution)/shard_map/all_gather | solution.py:76
  234.3 6.6 %fusion.3 = bf16[1,512,512]{2,1,0:T(8,128)(2,1)} fusion(bf16[512,4096]{0,1:T(8,128)(2,1)} %all-gather.6.cloned.1.call-done, bf16[4096,512]{1,0:T(8,128)(2,1)} %all-gather.8.cloned.1.call-done, bf16[1,512,512]{2,1,0:T(8,128)(2,1)S(1)} %copy-done.2), kind=kOutput, calls=%fused_computation.8 | convolution fusion | flops 2148270080 | bytes 9437184 | tf_op jit(solution)/shard_map/dot_general | solution.py:77
  (108 shorter events, 5.3 us)
Async XLA Ops:
  6.5 37.7 %copy-start = (bf16[1,512,256]{2,1,0:T(8,128)(2,1)S(1)}, bf16[1,512,256]{2,1,0:T(8,128)(2,1)}, u32[]{:S(2)}) copy-start(bf16[1,512,256]{2,1,0:T(8,128)(2,1)} %param.10) | copy-start | bytes 786436
  6.5 90.4 %all-gather.10.cloned.1.call-start = ((), (), s32[]{:S(2)}) async-start(), calls=%async_computation.2 | async-start | bytes 2162688 | tf_op jit(solution)/shard_map/all_gather | solution.py:12
  11.8 174.0 %all-gather.8.cloned.1.call-start = ((), (), s32[]{:S(2)}) async-start(), calls=%async_computation.1 | async-start | bytes 4325376 | tf_op jit(solution)/shard_map/all_gather | solution.py:79
  12.6 221.7 %all-gather.6.cloned.1.call-start = ((), (), s32[]{:S(2)}) async-start(), calls=%async_computation | async-start | bytes 4456448 | tf_op jit(solution)/shard_map/all_gather | solution.py:76
  134.2 1.1 copy-start.1
  134.2 100.1 %copy-start.2 = (bf16[1,512,512]{2,1,0:T(8,128)(2,1)S(1)}, bf16[1,512,512]{2,1,0:T(8,128)(2,1)}, u32[]{:S(2)}) copy-start(bf16[1,512,512]{2,1,0:T(8,128)(2,1)} %param.17) | copy-start | bytes 1572868
Sparse Core Ops, SparseCore 0:
  11.9 85.0 all-gather.9
  100.1 85.6 all-gather.7
  187.9 46.2 all-gather.5
where the time goes:
time: 249 us; the launch traced here: 247 us
  waiting for transfers between devices  152 us (61%)
  other arithmetic  33 us (13%)
  blocking collectives  31.4 us (13%)
  between operations  13.2 us (5%)
  matrix products  8.93 us (4%)
  local copies, waits for them, and re-layouts  8.36 us (3%)
    all_gather x1, waiting for transfers between devices, prefix_2(): lax.all_gather(part.astype(kind), axis)  52.7 us
    all_gather x1, waiting for transfers between devices, local(): lax.all_gather(out_weight, 'context', axis=0, tiled=True)  49.7 us
    all_gather x1, waiting for transfers between devices, local(): all_heads = lax.all_gather(normed, 'tensor', axis=1, tiled=True)  48.4 us
    all_gather x1, blocking collectives, prefix_2(): lax.all_gather(part.astype(kind), axis)  31.4 us
    select_n x32, other arithmetic, lap(): return jax.tree.map(lambda a, b: jnp.where(reached, a, b), new, before)  29.7 us
    dot_general x1, matrix products, local(): jnp.dot(all_heads, lax.all_gather(out_weight, 'context', axis=0, tiled=Tr...  6.61 us
    dynamic_slice x64, local copies, waits for them, and re-layouts, lap(): part[k].astype(own.dtype)  6.03 us
  transfers between devices with their start and end apart: 3, of which 3 were waited for; matrix products, arithmetic and copies ran while one was open for 16% of the time, Pallas kernels for 0%

commit v1 on v0

v1 whole, which is shorter than its diff:
```python
import functools

import jax
import jax.numpy as jnp
from jax import lax
from jax.experimental import pallas as pl
from jax.experimental.pallas import tpu as pltpu
from jax.sharding import PartitionSpec as P

MESH = pl.DeviceIdType.MESH
NX = 4
EPSILON = 1e-06
F32 = jnp.float32
BF16 = jnp.bfloat16
NT = (((1,), (1,)), ((), ()))
TN = (((0,), (0,)), ((), ()))


class Net:
    def __init__(self, send_sem, recv_sem):
        self.send_sem, self.recv_sem = send_sem, recv_sem
        self.number = {}
        self.sent = []

    def slot(self, name):
        return self.number.setdefault(name, len(self.number))

    def copy(self, name, src, dst, target):
        i = self.slot(name)
        return pltpu.make_async_remote_copy(
            src_ref=src,
            dst_ref=dst,
            send_sem=self.send_sem.at[i],
            recv_sem=self.recv_sem.at[i],
            device_id=target,
            device_id_type=MESH,
        )

    def send(self, name, src, dst, target, when=None):
        copy = self.copy(name, src, dst, target)
        if when is None:
            copy.start()
        else:
            pl.when(when)(copy.start)
        self.sent.append((copy, when))

    def arrive(self, name, place, source, when=None):
        copy = self.copy(name, place, place, source)
        if when is None:
            copy.wait_recv()
        else:
            pl.when(when)(copy.wait_recv)

    def drain(self):
        for copy, when in self.sent:
            if when is None:
                copy.wait_send()
            else:
                pl.when(when)(copy.wait_send)


def kernel(
    dims,
    q_hbm, k_hbm, cnt_hbm, scale_ref, ld_ref, gain_ref, w_hbm, res_hbm, out_hbm,
    q, k, cnt, res, v, acc, out, tri, col, intra, a_all, w_all,
    p1_send, p1_recv, p2_send, p2_recv, p3_send, p3_recv,
    send_sem, recv_sem, load_sem,
):
    ny, nz, heads, hs, block, wrows, xr = dims
    ctx, ten = lax.axis_index("context"), lax.axis_index("tensor")
    y, x = ctx // NX, ctx % NX
    z, core = ten // 2, ten % 2
    quarter = hs // NX
    half = block // 2
    ry, rz = ny // 2, nz // 2
    yr = wrows - xr

    def yp(d):
        return lax.rem(y + (d + ny), ny)

    def xp(d):
        return lax.rem(x + (d + NX), NX)

    def zp(d):
        return lax.rem(z + (d + nz), nz)

    def at_y(d):
        return (yp(d) * NX + x, ten)

    def at_x(d):
        return (y * NX + xp(d), ten)

    def at_z(d):
        return (ctx, zp(d) * 2 + core)

    partner = (ctx, z * 2 + (1 - core))
    net = Net(send_sem, recv_sem)

    loads = [
        pltpu.make_async_copy(k_hbm.at[0], k, load_sem.at[0]),
        pltpu.make_async_copy(cnt_hbm.at[0], cnt, load_sem.at[1]),
        pltpu.make_async_copy(w_hbm, w_all.at[ctx], load_sem.at[2]),
        pltpu.make_async_copy(q_hbm.at[0], q, load_sem.at[3]),
        pltpu.make_async_copy(res_hbm.at[0], res, load_sem.at[4]),
    ]
    for load in loads:
        load.start()
    barrier = pltpu.get_barrier_semaphore()
    friends = [at_y(d) for d in range(1, ny)] + [at_x(d) for d in range(1, NX)]
    friends += [at_z(1), at_z(-1), partner]
    for friend in friends:
        pl.semaphore_signal(barrier, inc=1, device_id=friend, device_id_type=MESH)

    t_index = lax.broadcasted_iota(jnp.int32, (block, block), 0)
    s_index = lax.broadcasted_iota(jnp.int32, (block, block), 1)
    tri[...] = jnp.where(t_index >= s_index, 1.0, 0.0).astype(BF16)

    def parts(value):
        hi = value.astype(BF16)
        rest = value - hi.astype(F32)
        mid = rest.astype(BF16)
        return hi, mid, (rest - mid.astype(F32)).astype(BF16)

    for h in range(heads):
        total = None
        for part in parts(jnp.broadcast_to(ld_ref[0, h : h + 1, :], (hs, block))):
            term = lax.dot_general(tri[...], part, NT, preferred_element_type=F32)
            total = term if total is None else total + term
        col[h] = total
    rates = jnp.concatenate([ld_ref[0, 0:heads, :]] * (8 // heads), axis=0)
    row = None
    for part in parts(rates):
        term = lax.dot_general(part, tri[...], NT, preferred_element_type=F32)
        row = term if row is None else row + term

    loads[0].wait()
    loads[1].wait()
    v[...] = (cnt[...].astype(F32) * scale_ref[...]).astype(BF16)

    def decay_rows(decays):
        index = lax.broadcasted_iota(jnp.int32, (16, hs), 0)
        rows = jnp.zeros((16, hs), F32)
        for h, decay in enumerate(decays):
            hi = decay.astype(BF16).astype(F32)
            rows = jnp.where(index == 2 * h, hi, rows)
            rows = jnp.where(index == 2 * h + 1, decay - hi, rows)
        return rows.astype(BF16)

    def read_decays(tile):
        rows = tile.astype(F32)
        return [rows[2 * h : 2 * h + 1, :] + rows[2 * h + 1 : 2 * h + 2, :] for h in range(heads)]

    depth = heads * quarter
    own_decay = []
    for h in range(heads):
        lanes = slice(h * hs, (h + 1) * hs)
        last = col[h, block - 1 : block, :]
        to_end = jnp.exp(last - col[h])
        weighted = (k[:, lanes].astype(F32) * to_end).astype(BF16)
        state = lax.dot_general(weighted, v[:, lanes], TN, preferred_element_type=F32)
        for part in range(NX):
            p1_send[part, h * quarter : (h + 1) * quarter, :] = state[
                part * quarter : (part + 1) * quarter, :
            ].astype(BF16)
        own_decay.append(jnp.exp(last))
    own_rows = decay_rows(own_decay)
    for part in range(NX):
        p1_send[part, depth : depth + 16, :] = own_rows

    pl.semaphore_wait(barrier, len(friends))

    for d in (2, 1, 3):
        net.send(("p1", d), p1_send.at[xp(d)], p1_recv.at[x], at_x(d))
    p1_recv[pl.ds(x, 1)] = p1_send[pl.ds(x, 1)]

    def w_x(c, rows=slice(0, xr)):
        return w_all.at[c, pl.ds(rows.start, rows.stop - rows.start), :]

    def w_y(c, lo=xr, hi=wrows):
        return w_all.at[c, pl.ds(lo, hi - lo), :]

    def bundle(d, lo=0, hi=NX):
        return w_all.at[pl.ds(yp(d) * NX + lo, hi - lo), pl.ds(0, xr), :]

    x_lo, x_hi = slice(0, xr // 32 * 16), slice(xr // 32 * 16, xr)
    y_mid = xr + yr // 32 * 16

    def c_at(dy, dx):
        return yp(dy) * NX + xp(dx)

    def y1_send(step):
        if step < ry:
            net.send(("y1", step, 1), w_y(c_at(1 - step, 0)), w_y(c_at(1 - step, 0)), at_y(1))
            net.send(("y1", step, -1), w_y(c_at(step - 1, 0)), w_y(c_at(step - 1, 0)), at_y(-1))
        else:
            net.send(("y1", step, 1), w_y(c_at(1 - step, 0), xr, y_mid), w_y(c_at(1 - step, 0), xr, y_mid), at_y(1))
            net.send(("y1", step, -1), w_y(c_at(step - 1, 0), y_mid), w_y(c_at(step - 1, 0), y_mid), at_y(-1))

    def y1_wait(step):
        if step < ry:
            net.arrive(("y1", step, 1), w_y(c_at(-step, 0)), at_y(-1))
            net.arrive(("y1", step, -1), w_y(c_at(step, 0)), at_y(1))
        else:
            net.arrive(("y1", step, 1), w_y(c_at(-step, 0), xr, y_mid), at_y(-1))
            net.arrive(("y1", step, -1), w_y(c_at(step, 0), y_mid), at_y(1))

    def y2_send(d):
        for way in (1, -1):
            net.send(("y2", d, way), w_y(c_at(d, 0)), w_y(c_at(d, 0)), at_x(way))

    def y2_relay(d):
        for way in (1, -1):
            net.arrive(("y2", d, way), w_y(c_at(d, -way)), at_x(-way))
        way = 1 if 0 <= d < ry else -1
        net.send(("y3", d), w_y(c_at(d, -way)), w_y(c_at(d, -way)), at_x(way))

    def y3_wait(d):
        way = 1 if 0 <= d < ry else -1
        net.arrive(("y3", d), w_y(c_at(d, 2)), at_x(-way))

    def x1_send():
        for way in (1, -1):
            net.send(("x1", way), w_x(ctx), w_x(ctx), at_x(way))

    def x1_relay():
        for way in (1, -1):
            net.arrive(("x1", way), w_x(c_at(0, -way)), at_x(-way))
        for way, rows in ((1, x_lo), (-1, x_hi)):
            net.send(("x1r", way), w_x(c_at(0, -way), rows), w_x(c_at(0, -way), rows), at_x(way))

    def x1_wait():
        for way, rows in ((1, x_lo), (-1, x_hi)):
            net.arrive(("x1r", way), w_x(c_at(0, 2), rows), at_x(-way))

    def x2_range(step, way):
        if step < ry:
            return 0, NX
        return (0, NX // 2) if way == 1 else (NX // 2, NX)

    def x2_send(step):
        for way in (1, -1):
            part = bundle(way * (1 - step), *x2_range(step, way))
            net.send(("x2", step, way), part, part, at_y(way))

    def x2_wait(step):
        for way in (1, -1):
            net.arrive(("x2", step, way), bundle(-way * step, *x2_range(step, way)), at_y(-way))

    strip = block // 4
    s_in = lax.broadcasted_iota(jnp.int32, (strip, strip), 1)
    t_in = lax.broadcasted_iota(jnp.int32, (strip, strip), 0)

    def attend(h):
        lanes = slice(h * hs, (h + 1) * hs)
        for i in range(4):
            rows, upto = slice(i * strip, (i + 1) * strip), (i + 1) * strip
            scores = lax.dot_general(q[rows, lanes], k[0:upto, lanes], NT, preferred_element_type=F32)
            here = col[h, rows, 0:1]
            pieces = []
            for j in range(i + 1):
                gap = here - row[h : h + 1, j * strip : (j + 1) * strip]
                if j == i:
                    gap = jnp.where(t_in >= s_in, gap, -1e30)
                pieces.append((scores[:, j * strip : (j + 1) * strip] * jnp.exp(gap)).astype(BF16))
            weights = jnp.concatenate(pieces, axis=1) if i else pieces[0]
            intra[h, rows, :] = jnp.dot(weights, v[0:upto, lanes], preferred_element_type=F32)

    loads[2].wait()
    x1_send()
    y1_send(1)
    loads[3].wait()
    attend(0)

    for d in range(1, NX):
        net.arrive(("p1", d), p1_recv.at[xp(-d)], at_x(-d))
    inside, before = [], []
    run = [jnp.zeros((quarter, hs), F32) for _ in range(heads)]
    run_decay = [jnp.ones((1, hs), F32) for _ in range(heads)]
    for i in range(NX):
        inside.append(run)
        before.append(run_decay)
        decays = read_decays(p1_recv[i, depth : depth + 16, :])
        states = [p1_recv[i, h * quarter : (h + 1) * quarter, :].astype(F32) for h in range(heads)]
        run = [run[h] * decays[h] + states[h] for h in range(heads)]
        run_decay = [run_decay[h] * decays[h] for h in range(heads)]
    for h in range(heads):
        p2_send[h * quarter : (h + 1) * quarter, :] = run[h].astype(BF16)
    p2_send[depth : depth + 16, :] = decay_rows(run_decay)
    for d in sorted(range(1, ny), key=lambda d: -min(d, ny - d)):
        net.send(("p2", d), p2_send, p2_recv.at[d - 1], at_y(d), when=y + d < ny)

    x1_relay()
    y2_send(0)
    y1_wait(1)
    y2_send(1)
    y2_send(-1)
    attend(1)

    for d in range(1, ny):
        net.arrive(("p2", d), p2_recv.at[d - 1], at_y(-d), when=y >= d)
    rows_before = [jnp.zeros((quarter, hs), F32) for _ in range(heads)]
    for d in range(ny - 1, 0, -1):
        there = y >= d
        decays = read_decays(p2_recv[d - 1, depth : depth + 16, :])
        for h in range(heads):
            state = p2_recv[d - 1, h * quarter : (h + 1) * quarter, :].astype(F32)
            rows_before[h] = jnp.where(there, rows_before[h] * decays[h] + state, 0.0)
    for i in range(NX):
        for h in range(heads):
            p3_send[i, h * quarter : (h + 1) * quarter, :] = (
                rows_before[h] * before[i][h] + inside[i][h]
            ).astype(BF16)
    for d in (2, 1, 3):
        net.send(("p3", d), p3_send.at[xp(d)], p3_recv.at[x], at_x(d))
    p3_recv[pl.ds(x, 1)] = p3_send[pl.ds(x, 1)]
    y1_send(2)
    x1_wait()
    x2_send(1)
    y2_relay(0)

    for d in range(1, NX):
        net.arrive(("p3", d), p3_recv.at[xp(-d)], at_x(-d))

    def piece(t, part):
        return a_all.at[t, pl.ds(part * half, half), :]

    def z_item(i, way):
        return -way * (i // 2), (i % 2 if way == 1 else 1 - i % 2)

    def z_send(i, way):
        d, part = z_item(i, way)
        own = piece(zp(d) * 2 + core, part)
        net.send(("z", i, way), own, own, at_z(way))

    def z_wait(i, way):
        d, part = z_item(i, way)
        net.arrive(("z", i, way), piece(zp(d - way) * 2 + core, part), at_z(-way))

    def hand(d, part):
        own = piece(zp(d) * 2 + core, part)
        net.send(("hand", d, part), own, own, partner)

    def hand_wait(d, part):
        net.arrive(("hand", d, part), piece(zp(d) * 2 + (1 - core), part), partner)

    incoming = [
        jnp.concatenate([p3_recv[i, h * quarter : (h + 1) * quarter, :] for i in range(NX)], axis=0)
        for h in range(heads)
    ]
    for part in range(2):
        rows = slice(part * half, (part + 1) * half)
        for h in range(heads):
            lanes = slice(h * hs, (h + 1) * hs)
            carried = jnp.dot(q[rows, lanes], incoming[h], preferred_element_type=F32)
            mixed = intra[h, rows, :] + jnp.exp(col[h, rows, :]) * carried
            scale = lax.rsqrt(jnp.mean(mixed * mixed, axis=1, keepdims=True) + EPSILON)
            a_all[ten, rows, lanes] = (mixed * scale * gain_ref[:, lanes]).astype(BF16)
        z_send(part, 1)
        z_send(1 - part, -1) if part else None
    z_send(1, -1)
    hand(0, 0)
    hand(0, 1)

    w_events = [
        [lambda: y1_wait(2), lambda: y1_send(3), lambda: y2_send(2), lambda: y2_send(-2),
         lambda: y2_relay(1), lambda: y2_relay(-1), lambda: x2_wait(1), lambda: x2_send(2)],
        [lambda: y1_wait(3), lambda: y1_send(4), lambda: y2_send(3), lambda: y2_send(-3),
         lambda: y2_relay(2), lambda: y2_relay(-2), lambda: x2_wait(2), lambda: x2_send(3)],
        [lambda: y1_wait(4), lambda: y2_send(4), lambda: y2_relay(3), lambda: y2_relay(-3),
         lambda: x2_wait(3), lambda: x2_send(4)],
        [lambda: y2_relay(4)],
        [lambda: x2_wait(4)] + [functools.partial(y3_wait, d) for d in (0, 1, -1, 2, -2, 3, -3, 4)],
    ]

    def multiply(d, part, first=False):
        rows = pl.ds(part * half, half)
        base = zp(d)
        result = None
        for c in range(2):
            weight = w_all[pl.ds(base * 4 + 2 * c, 2)].reshape(2 * wrows, -1)
            term = jnp.dot(a_all[base * 2 + c, rows, :], weight, preferred_element_type=F32)
            result = term if result is None else result + term
        if first:
            acc[rows, :] = result
        else:
            acc[rows, :] += result

    last = 2 * rz - 2
    for i in range(last + 1):
        for way in (1, -1):
            z_wait(i, way)
            if i + 2 <= last:
                z_send(i + 2, way)
            d, part = z_item(i, way)
            hand(d - way, part)
        if i < len(w_events):
            for event in w_events[i]:
                event()
        if i == 4:
            hand_wait(0, 0)
            hand_wait(0, 1)
            multiply(0, 0, True)
            multiply(0, 1, True)
            for d in (-1, 1, -2, 2):
                for part in range(2):
                    hand_wait(d, part)
                    multiply(d, part)
        if i == 5:
            for d in (-3, 3):
                for part in range(2):
                    hand_wait(d, part)
                    multiply(d, part)
    loads[4].wait()
    stores = []
    for part in range(2):
        rows = pl.ds(part * half, half)
        d = -4 if part == 0 else 4
        hand_wait(d, part)
        multiply(d, part)
        out[rows, :] = (res[rows, :].astype(F32) + acc[rows, :]).astype(BF16)
        stores.append(pltpu.make_async_copy(out.at[rows, :], out_hbm.at[0, rows, :], load_sem.at[5 + part]))
        stores[-1].start()
    for store in stores:
        store.wait()
    net.drain()


def local(dims, queries, keys, spike_counts, spike_scale, log_decay, norm_gain, out_weight, residual_in):
    ny, nz, heads, hs, block, wrows, xr = dims
    width = heads * hs
    columns = out_weight.shape[1]
    depth = heads * hs // NX + 16
    vmem = pl.BlockSpec(memory_space=pltpu.VMEM)
    hbm = pl.BlockSpec(memory_space=pl.ANY)
    return pl.pallas_call(
        functools.partial(kernel, dims),
        out_shape=jax.ShapeDtypeStruct((1, block, columns), BF16),
        in_specs=[hbm, hbm, hbm, vmem, vmem, vmem, hbm, hbm],
        out_specs=hbm,
        scratch_shapes=[
            pltpu.VMEM((block, width), BF16),
            pltpu.VMEM((block, width), BF16),
            pltpu.VMEM((block, width), jnp.int32),
            pltpu.VMEM((block, columns), BF16),
            pltpu.VMEM((block, width), BF16),
            pltpu.VMEM((block, columns), F32),
            pltpu.VMEM((block, columns), BF16),
            pltpu.VMEM((block, block), BF16),
            pltpu.VMEM((heads, block, hs), F32),
            pltpu.VMEM((heads, block, hs), F32),
            pltpu.VMEM((2 * nz, block, width), BF16),
            pltpu.VMEM((ny * NX, wrows, columns), BF16),
            pltpu.VMEM((NX, depth, hs), BF16),
            pltpu.VMEM((NX, depth, hs), BF16),
            pltpu.VMEM((depth, hs), BF16),
            pltpu.VMEM((ny - 1, depth, hs), BF16),
            pltpu.VMEM((NX, depth - 16, hs), BF16),
            pltpu.VMEM((NX, depth - 16, hs), BF16),
            pltpu.SemaphoreType.DMA((96,)),
            pltpu.SemaphoreType.DMA((96,)),
            pltpu.SemaphoreType.DMA((8,)),
        ],
        compiler_params=pltpu.CompilerParams(
            collective_id=0, has_side_effects=True, vmem_limit_bytes=40 * 1024 * 1024
        ),
    )(
        queries, keys, spike_counts, spike_scale.reshape(1, width), log_decay,
        norm_gain.reshape(1, width), out_weight, residual_in,
    )


def solution(mesh):
    ny, nz = mesh.shape["context"] // NX, mesh.shape["tensor"] // 2

    def whole(queries, keys, spike_counts, spike_scale, log_decay, norm_gain, out_weight, residual_in):
        heads = log_decay.shape[1] // (2 * nz)
        hs = queries.shape[2] // log_decay.shape[1]
        block = queries.shape[1] // (ny * NX)
        wrows = out_weight.shape[0] // (ny * NX)
        xr = wrows * 3 // 8
        dims = (ny, nz, heads, hs, block, wrows, xr)
        in_specs = (
            P(None, "context", "tensor"),
            P(None, "context", "tensor"),
            P(None, "context", "tensor"),
            P("tensor"),
            P(None, "tensor", "context"),
            P("tensor"),
            P("context", "tensor"),
            P(None, "context", "tensor"),
        )
        return jax.shard_map(
            functools.partial(local, dims),
            mesh=mesh,
            in_specs=in_specs,
            out_specs=P(None, "context", "tensor"),
            check_vma=False,
        )(queries, keys, spike_counts, spike_scale, log_decay, norm_gain, out_weight, residual_in)

    return whole
```

time: 249 us -> 66.7 us (0.27)
  waiting for transfers between devices: 152 us -> 0 us
  Pallas kernels: 0 us -> 59.3 us
  other arithmetic: 33 us -> 0 us
  blocking collectives: 31.4 us -> 0 us
  between operations: 13.2 us -> 0.02 us
  matrix products: 8.93 us -> 0 us
    all_gather x3 -> x0, waiting for transfers between devices: 151 us -> none  [the longest x1 52.7 us: prefix_2(): lax.all_gather(part.astype(kind), axis)]
    pallas_call x0 -> x1, Pallas kernels: none -> 59.3 us  [local(): pl.pallas_call(functools.partial(kernel, dims), out_shape=jax.ShapeDtypeS...]
    all_gather x1 -> x0, blocking collectives: 31.4 us -> none  [prefix_2(): lax.all_gather(part.astype(kind), axis)]
    select_n x32 -> x0, other arithmetic: 29.7 us -> none  [lap(): return jax.tree.map(lambda a, b: jnp.where(reached, a, b), new, before)]
    dot_general x4 -> x0, matrix products: 8.93 us -> none  [the longest x1 6.61 us: local(): jnp.dot(all_heads, lax.all_gather(out_weight, 'context', axis=0, tiled=Tr...]
    unnamed x7 -> x17, local copies, waits for them, and re-layouts: 0.09 us -> 7.06 us
    dynamic_slice x64 -> x0, local copies, waits for them, and re-layouts: 6.03 us -> none  [lap(): part[k].astype(own.dtype)]
  transfers between devices with their start and end apart: 3 -> 0, of which waited for: 3 -> 0; matrix products, arithmetic and copies ran while one was open for 16% -> 0% of each run, Pallas kernels for 0% -> 0%
where the time goes in v1:
time: 66.7 us; the launch traced here: 66.4 us
  Pallas kernels  59.3 us (89%)
  local copies, waits for them, and re-layouts  7.06 us (11%)
    pallas_call x1, Pallas kernels, local(): pl.pallas_call(functools.partial(kernel, dims), out_shape=jax.ShapeDtypeS...  59.3 us
    unnamed x17, local copies, waits for them, and re-layouts  7.06 us

profile of v1, /device:TPU:1, one launch (start us, length us, event | category | flops | bytes accessed | tf_op | source)
XLA Modules:
  0.0 66.4 jit_solution(4678912588424324293)
XLA Ops:
  0.0 0.0 copy-start.7
  0.0 0.0 copy-start.6
  0.0 0.7 %copy-done.7 = f32[256]{0:T(256)S(1)} copy-done((f32[256]{0:T(256)S(1)}, f32[256]{0:T(256)}, u32[]{:S(2)}) %copy-start.7) | copy-done | bytes 1048
  0.7 0.0 copy-done.6
  0.7 0.0 copy-start
  0.7 1.0 %copy-done = s32[1,512,256]{2,1,0:T(8,128)S(1)} copy-done((s32[1,512,256]{2,1,0:T(8,128)S(1)}, s32[1,512,256]{2,1,0:T(8,128)}, u32[]{:S(2)}) %copy-start) | copy-done | bytes 524312
  1.7 0.0 copy-start.1
  1.7 1.0 %copy-done.1 = bf16[1,512,512]{2,1,0:T(8,128)(2,1)S(1)} copy-done((bf16[1,512,512]{2,1,0:T(8,128)(2,1)S(1)}, bf16[1,512,512]{2,1,0:T(8,128)(2,1)}, u32[]{:S(2)}) %copy-start.1) | copy-done | bytes 524312
  2.8 0.0 copy-start.2
  2.8 0.9 %copy-done.2 = bf16[1,512,256]{2,1,0:T(8,128)(2,1)S(1)} copy-done((bf16[1,512,256]{2,1,0:T(8,128)(2,1)S(1)}, bf16[1,512,256]{2,1,0:T(8,128)(2,1)}, u32[]{:S(2)}) %copy-start.2) | copy-done | bytes 262168
  3.7 0.0 copy-start.3
  3.7 0.9 %copy-done.3 = bf16[1,512,256]{2,1,0:T(8,128)(2,1)S(1)} copy-done((bf16[1,512,256]{2,1,0:T(8,128)(2,1)S(1)}, bf16[1,512,256]{2,1,0:T(8,128)(2,1)}, u32[]{:S(2)}) %copy-start.3) | copy-done | bytes 262168
  4.7 0.0 copy-start.4
  4.7 0.9 %copy-done.4 = bf16[128,512]{1,0:T(8,128)(2,1)S(1)} copy-done((bf16[128,512]{1,0:T(8,128)(2,1)S(1)}, bf16[128,512]{1,0:T(8,128)(2,1)}, u32[]{:S(2)}) %copy-start.4) | copy-done | bytes 131096
  5.6 0.0 copy-start.5
  5.6 0.7 %copy-done.5 = f32[1,2,512]{2,1,0:T(2,128)S(1)} copy-done((f32[1,2,512]{2,1,0:T(2,128)S(1)}, f32[1,2,512]{2,1,0:T(2,128)}, u32[]{:S(2)}) %copy-start.5) | copy-done | bytes 4120
  6.3 59.3 %shard_map.82 = bf16[1,512,512]{2,1,0:T(8,128)(2,1)S(1)} custom-call(bf16[1,512,256]{2,1,0:T(8,128)(2,1)S(1)} %copy-done.2, bf16[1,512,256]{2,1,0:T(8,128)(2,1)S(1)} %copy-done.3, s32[1,512,256]{2,1,0:T(8,128)S(1)} %copy-done, f32[1,256]{1,0:T(1,128)S(1)} %bitcast.2, f32[1,2,512]{2,1,0:T(2,128)S(1)} %copy-done.5, f32[1,256]{1,0:T(1,128)S(1)} %bitcast.3, ...), custom_call_target="tpu_custom_call" | custom-call | tf_op jit(solution)/shard_map/pallas_call | solution.py:435
  65.6 0.8 %copy.10 = bf16[1,512,512]{2,1,0:T(8,128)(2,1)} copy(bf16[1,512,512]{2,1,0:T(8,128)(2,1)S(1)} %shard_map.82) | data formatting | bytes 1048576
Async XLA Ops:
  0.0 0.7 %copy-start.7 = (f32[256]{0:T(256)S(1)}, f32[256]{0:T(256)}, u32[]{:S(2)}) copy-start(f32[256]{0:T(256)} %param.13) | copy-start | bytes 3076
  0.0 0.7 %copy-start.6 = (f32[256]{0:T(256)S(1)}, f32[256]{0:T(256)}, u32[]{:S(2)}) copy-start(f32[256]{0:T(256)} %param.11) | copy-start | bytes 3076
  0.7 1.0 %copy-start = (s32[1,512,256]{2,1,0:T(8,128)S(1)}, s32[1,512,256]{2,1,0:T(8,128)}, u32[]{:S(2)}) copy-start(s32[1,512,256]{2,1,0:T(8,128)} %cnt_hbm.1) | copy-start | bytes 1572868
  1.7 1.0 %copy-start.1 = (bf16[1,512,512]{2,1,0:T(8,128)(2,1)S(1)}, bf16[1,512,512]{2,1,0:T(8,128)(2,1)}, u32[]{:S(2)}) copy-start(bf16[1,512,512]{2,1,0:T(8,128)(2,1)} %res_hbm.1) | copy-start | bytes 1572868
  2.8 0.9 %copy-start.2 = (bf16[1,512,256]{2,1,0:T(8,128)(2,1)S(1)}, bf16[1,512,256]{2,1,0:T(8,128)(2,1)}, u32[]{:S(2)}) copy-start(bf16[1,512,256]{2,1,0:T(8,128)(2,1)} %q_hbm.1) | copy-start | bytes 786436
  3.7 0.9 %copy-start.3 = (bf16[1,512,256]{2,1,0:T(8,128)(2,1)S(1)}, bf16[1,512,256]{2,1,0:T(8,128)(2,1)}, u32[]{:S(2)}) copy-start(bf16[1,512,256]{2,1,0:T(8,128)(2,1)} %k_hbm.1) | copy-start | bytes 786436
  4.7 0.9 %copy-start.4 = (bf16[128,512]{1,0:T(8,128)(2,1)S(1)}, bf16[128,512]{1,0:T(8,128)(2,1)}, u32[]{:S(2)}) copy-start(bf16[128,512]{1,0:T(8,128)(2,1)} %w_hbm.1) | copy-start | bytes 393220
  5.6 0.7 %copy-start.5 = (f32[1,2,512]{2,1,0:T(2,128)S(1)}, f32[1,2,512]{2,1,0:T(2,128)}, u32[]{:S(2)}) copy-start(f32[1,2,512]{2,1,0:T(2,128)} %ld_ref.1) | copy-start | bytes 12292

commit v2 on v1

--- a/solution.py
+++ b/solution.py
@@ -61,8 +61,8 @@
 
 def kernel(
     dims,
-    q_hbm, k_hbm, cnt_hbm, scale_ref, ld_ref, gain_ref, w_hbm, res_hbm, out_hbm,
-    q, k, cnt, res, v, acc, out, tri, col, intra, a_all, w_all,
+    q_hbm, k_hbm, cnt_hbm, scale_hbm, ld_hbm, gain_hbm, w_hbm, res_hbm, out_ref,
+    q, k, cnt, scale_ref, ld_ref, gain_ref, res, v, acc, tri, col, intra, a_all, w_all,
     p1_send, p1_recv, p2_send, p2_recv, p3_send, p3_recv,
     send_sem, recv_sem, load_sem,
 ):
@@ -102,9 +102,12 @@
         pltpu.make_async_copy(w_hbm, w_all.at[ctx], load_sem.at[2]),
         pltpu.make_async_copy(q_hbm.at[0], q, load_sem.at[3]),
         pltpu.make_async_copy(res_hbm.at[0], res, load_sem.at[4]),
+        pltpu.make_async_copy(ld_hbm, ld_ref, load_sem.at[5]),
+        pltpu.make_async_copy(scale_hbm, scale_ref, load_sem.at[6]),
+        pltpu.make_async_copy(gain_hbm, gain_ref, load_sem.at[7]),
     ]
-    for load in loads:
-        load.start()
+    for i in (5, 6, 0, 1, 2, 3, 7, 4):
+        loads[i].start()
     barrier = pltpu.get_barrier_semaphore()
     friends = [at_y(d) for d in range(1, ny)] + [at_x(d) for d in range(1, NX)]
     friends += [at_z(1), at_z(-1), partner]
@@ -121,6 +124,7 @@
         mid = rest.astype(BF16)
         return hi, mid, (rest - mid.astype(F32)).astype(BF16)
 
+    loads[5].wait()
     for h in range(heads):
         total = None
         for part in parts(jnp.broadcast_to(ld_ref[0, h : h + 1, :], (hs, block))):
@@ -135,6 +139,7 @@
 
     loads[0].wait()
     loads[1].wait()
+    loads[6].wait()
     v[...] = (cnt[...].astype(F32) * scale_ref[...]).astype(BF16)
 
     def decay_rows(decays):
@@ -347,6 +352,7 @@
         jnp.concatenate([p3_recv[i, h * quarter : (h + 1) * quarter, :] for i in range(NX)], axis=0)
         for h in range(heads)
     ]
+    loads[7].wait()
     for part in range(2):
         rows = slice(part * half, (part + 1) * half)
         for h in range(heads):
@@ -411,17 +417,12 @@
                     hand_wait(d, part)
                     multiply(d, part)
     loads[4].wait()
-    stores = []
     for part in range(2):
         rows = pl.ds(part * half, half)
         d = -4 if part == 0 else 4
         hand_wait(d, part)
         multiply(d, part)
-        out[rows, :] = (res[rows, :].astype(F32) + acc[rows, :]).astype(BF16)
-        stores.append(pltpu.make_async_copy(out.at[rows, :], out_hbm.at[0, rows, :], load_sem.at[5 + part]))
-        stores[-1].start()
-    for store in stores:
-        store.wait()
+        out_ref[0, rows, :] = (res[rows, :].astype(F32) + acc[rows, :]).astype(BF16)
     net.drain()
 
 
@@ -431,20 +432,22 @@
     columns = out_weight.shape[1]
     depth = heads * hs // NX + 16
     vmem = pl.BlockSpec(memory_space=pltpu.VMEM)
-    hbm = pl.BlockSpec(memory_space=pl.ANY)
+    hbm = pl.BlockSpec(memory_space=pltpu.HBM)
     return pl.pallas_call(
         functools.partial(kernel, dims),
-        out_shape=jax.ShapeDtypeStruct((1, block, columns), BF16),
-        in_specs=[hbm, hbm, hbm, vmem, vmem, vmem, hbm, hbm],
-        out_specs=hbm,
+        out_shape=pltpu.VMEM((1, block, columns), BF16),
+        in_specs=[hbm] * 8,
+        out_specs=vmem,
         scratch_shapes=[
             pltpu.VMEM((block, width), BF16),
             pltpu.VMEM((block, width), BF16),
             pltpu.VMEM((block, width), jnp.int32),
+            pltpu.VMEM((1, width), F32),
+            pltpu.VMEM((1, heads, block), F32),
+            pltpu.VMEM((1, width), F32),
             pltpu.VMEM((block, columns), BF16),
             pltpu.VMEM((block, width), BF16),
             pltpu.VMEM((block, columns), F32),
-            pltpu.VMEM((block, columns), BF16),
             pltpu.VMEM((block, block), BF16),
             pltpu.VMEM((heads, block, hs), F32),
             pltpu.VMEM((heads, block, hs), F32),
@@ -461,7 +464,7 @@
             pltpu.SemaphoreType.DMA((8,)),
         ],
         compiler_params=pltpu.CompilerParams(
-            collective_id=0, has_side_effects=True, vmem_limit_bytes=40 * 1024 * 1024
+            collective_id=0, has_side_effects=True, vmem_limit_bytes=60 * 1024 * 1024
         ),
     )(
         queries, keys, spike_counts, spike_scale.reshape(1, width), log_decay,

time: 66.7 us -> 59.9 us (0.90)
  local copies, waits for them, and re-layouts: 7.06 us -> 0.8 us
    unnamed x17 -> x1, local copies, waits for them, and re-layouts: 7.06 us -> 0.8 us
where the time goes in v2:
time: 59.9 us; the launch traced here: 59.8 us
  Pallas kernels  59 us (98%)
  local copies, waits for them, and re-layouts  0.8 us (1%)
    pallas_call x1, Pallas kernels, local(): pl.pallas_call(functools.partial(kernel, dims), out_shape=pltpu.VMEM((1,...  59 us

profile of v2, /device:TPU:1, one launch (start us, length us, event | category | flops | bytes accessed | tf_op | source)
XLA Modules:
  0.0 59.8 jit_solution(3932570104272179977)
XLA Ops:
  0.0 59.0 %shard_map.82 = bf16[1,512,512]{2,1,0:T(8,128)(2,1)S(1)} custom-call(bf16[1,512,256]{2,1,0:T(8,128)(2,1)} %q_hbm.1, bf16[1,512,256]{2,1,0:T(8,128)(2,1)} %k_hbm.1, s32[1,512,256]{2,1,0:T(8,128)} %cnt_hbm.1, f32[1,256]{1,0:T(1,128)} %bitcast.2, f32[1,2,512]{2,1,0:T(2,128)} %ld_hbm.1, f32[1,256]{1,0:T(1,128)} %bitcast.3, bf16[128,512]{1,0:T(8,128)(2,1)} %w_hbm.1, ...), custom_call_target="tpu_custom_call" | custom-call | tf_op jit(solution)/shard_map/pallas_call | solution.py:436
  59.0 0.8 %copy.10 = bf16[1,512,512]{2,1,0:T(8,128)(2,1)} copy(bf16[1,512,512]{2,1,0:T(8,128)(2,1)S(1)} %shard_map.82) | data formatting | bytes 1048576

commit v3 on v2

--- a/solution.py
+++ b/solution.py
@@ -14,6 +14,23 @@
 BF16 = jnp.bfloat16
 NT = (((1,), (1,)), ((), ()))
 TN = (((0,), (0,)), ((), ()))
+
+
+BEFORE_INCOMING = (
+    ("x1", 1), ("x1", -1), ("y1", 1, 1), ("y1", 1, -1), ("s2", 1), ("s2", -1), ("x1r", 1), ("x1r", -1),
+)
+BEFORE_MIXED = (
+    ("y2", 0, -1), ("y2", 0, 1), ("y1", 2, 1), ("y1", 2, -1), ("y2", 1, 1), ("y2", 1, -1), ("s2", -2), ("s2", 2),
+    ("y2", -1, 1), ("y2", -1, -1),
+)
+AFTER_MIXED = (
+    ("y3", 0), ("y2", -2, -1), ("x2", 1, -1), ("x2", 1, 1), ("y3", 1), ("y2", 2, -1), ("y1", 3, -1), ("s2", 3),
+    ("y1", 3, 1), ("s2", -3), ("y2", -2, 1), ("y3", -1), ("z", 0, -1), ("z", 0, 1), ("y2", 2, 1), ("y3", -2),
+    ("x2", 2, -1), ("x2", 2, 1), ("z", 1, -1), ("z", 1, 1), ("y2", 3, 1), ("y1", 4, 1), ("y2", 3, -1), ("y1", 4, -1),
+    ("s2", 4), ("y2", -3, 1), ("y2", -3, -1), ("z", 2, -1), ("z", 2, 1), ("y3", 2), ("y2", 4, -1), ("y3", 3),
+    ("x2", 3, -1), ("z", 3, -1), ("z", 3, 1), ("x2", 3, 1), ("y3", -3), ("y2", 4, 1), ("y3", 4), ("z", 4, -1),
+    ("z", 4, 1), ("x2", 4, -1), ("x2", 4, 1), ("z", 5, -1), ("z", 5, 1),
+)
 
 
 class Net:
@@ -62,7 +79,7 @@
 def kernel(
     dims,
     q_hbm, k_hbm, cnt_hbm, scale_hbm, ld_hbm, gain_hbm, w_hbm, res_hbm, out_ref,
-    q, k, cnt, scale_ref, ld_ref, gain_ref, res, v, acc, tri, col, intra, a_all, w_all,
+    q, k, cnt, scale_ref, ld_ref, gain_ref, res, v, acc, col, intra, a_all, w_all,
     p1_send, p1_recv, p2_send, p2_recv, p3_send, p3_recv,
     send_sem, recv_sem, load_sem,
 ):
@@ -114,9 +131,10 @@
     for friend in friends:
         pl.semaphore_signal(barrier, inc=1, device_id=friend, device_id_type=MESH)
 
-    t_index = lax.broadcasted_iota(jnp.int32, (block, block), 0)
-    s_index = lax.broadcasted_iota(jnp.int32, (block, block), 1)
-    tri[...] = jnp.where(t_index >= s_index, 1.0, 0.0).astype(BF16)
+    strip = block // 4
+    t_in = lax.broadcasted_iota(jnp.int32, (strip, strip), 0)
+    s_in = lax.broadcasted_iota(jnp.int32, (strip, strip), 1)
+    tri = jnp.where(t_in >= s_in, 1.0, 0.0).astype(BF16)
 
     def parts(value):
         hi = value.astype(BF16)
@@ -125,17 +143,23 @@
         return hi, mid, (rest - mid.astype(F32)).astype(BF16)
 
     loads[5].wait()
+    row = []
     for h in range(heads):
-        total = None
-        for part in parts(jnp.broadcast_to(ld_ref[0, h : h + 1, :], (hs, block))):
-            term = lax.dot_general(tri[...], part, NT, preferred_element_type=F32)
-            total = term if total is None else total + term
-        col[h] = total
-    rates = jnp.concatenate([ld_ref[0, 0:heads, :]] * (8 // heads), axis=0)
-    row = None
-    for part in parts(rates):
-        term = lax.dot_general(part, tri[...], NT, preferred_element_type=F32)
-        row = term if row is None else row + term
+        base, pieces = None, []
+        for i in range(4):
+            rates = ld_ref[0, h : h + 1, i * strip : (i + 1) * strip]
+            down = along = None
+            for part in parts(jnp.broadcast_to(rates, (hs, strip))):
+                term = lax.dot_general(tri, part, NT, preferred_element_type=F32)
+                down = term if down is None else down + term
+                term = lax.dot_general(part[0:16], tri, NT, preferred_element_type=F32)
+                along = term if along is None else along + term
+            if i:
+                down, along = down + base, along + base
+            col[h, i * strip : (i + 1) * strip, :] = down
+            base = down[strip - 1 : strip, :]
+            pieces.append(along[0:1, :])
+        row.append(jnp.concatenate(pieces, axis=1))
 
     loads[0].wait()
     loads[1].wait()
@@ -193,67 +217,70 @@
     def c_at(dy, dx):
         return yp(dy) * NX + xp(dx)
 
-    def y1_send(step):
+    def y1_part(step, way, d):
         if step < ry:
-            net.send(("y1", step, 1), w_y(c_at(1 - step, 0)), w_y(c_at(1 - step, 0)), at_y(1))
-            net.send(("y1", step, -1), w_y(c_at(step - 1, 0)), w_y(c_at(step - 1, 0)), at_y(-1))
-        else:
-            net.send(("y1", step, 1), w_y(c_at(1 - step, 0), xr, y_mid), w_y(c_at(1 - step, 0), xr, y_mid), at_y(1))
-            net.send(("y1", step, -1), w_y(c_at(step - 1, 0), y_mid), w_y(c_at(step - 1, 0), y_mid), at_y(-1))
-
-    def y1_wait(step):
-        if step < ry:
-            net.arrive(("y1", step, 1), w_y(c_at(-step, 0)), at_y(-1))
-            net.arrive(("y1", step, -1), w_y(c_at(step, 0)), at_y(1))
-        else:
-            net.arrive(("y1", step, 1), w_y(c_at(-step, 0), xr, y_mid), at_y(-1))
-            net.arrive(("y1", step, -1), w_y(c_at(step, 0), y_mid), at_y(1))
+            return w_y(c_at(d, 0))
+        return w_y(c_at(d, 0), xr, y_mid) if way == 1 else w_y(c_at(d, 0), y_mid)
+
+    def y1_send(step, way):
+        part = y1_part(step, way, way * (1 - step))
+        net.send(("y1", step, way), part, part, at_y(way))
 
     def y2_send(d):
         for way in (1, -1):
             net.send(("y2", d, way), w_y(c_at(d, 0)), w_y(c_at(d, 0)), at_x(way))
 
-    def y2_relay(d):
-        for way in (1, -1):
-            net.arrive(("y2", d, way), w_y(c_at(d, -way)), at_x(-way))
-        way = 1 if 0 <= d < ry else -1
-        net.send(("y3", d), w_y(c_at(d, -way)), w_y(c_at(d, -way)), at_x(way))
-
-    def y3_wait(d):
-        way = 1 if 0 <= d < ry else -1
-        net.arrive(("y3", d), w_y(c_at(d, 2)), at_x(-way))
+    def y3_way(d):
+        return 1 if 0 <= d < ry else -1
 
     def x1_send():
         for way in (1, -1):
             net.send(("x1", way), w_x(ctx), w_x(ctx), at_x(way))
 
-    def x1_relay():
-        for way in (1, -1):
-            net.arrive(("x1", way), w_x(c_at(0, -way)), at_x(-way))
-        for way, rows in ((1, x_lo), (-1, x_hi)):
-            net.send(("x1r", way), w_x(c_at(0, -way), rows), w_x(c_at(0, -way), rows), at_x(way))
-
-    def x1_wait():
-        for way, rows in ((1, x_lo), (-1, x_hi)):
-            net.arrive(("x1r", way), w_x(c_at(0, 2), rows), at_x(-way))
-
-    def x2_range(step, way):
+    def x2_part(step, way, d):
         if step < ry:
-            return 0, NX
-        return (0, NX // 2) if way == 1 else (NX // 2, NX)
-
-    def x2_send(step):
-        for way in (1, -1):
-            part = bundle(way * (1 - step), *x2_range(step, way))
-            net.send(("x2", step, way), part, part, at_y(way))
-
-    def x2_wait(step):
-        for way in (1, -1):
-            net.arrive(("x2", step, way), bundle(-way * step, *x2_range(step, way)), at_y(-way))
-
-    strip = block // 4
-    s_in = lax.broadcasted_iota(jnp.int32, (strip, strip), 1)
-    t_in = lax.broadcasted_iota(jnp.int32, (strip, strip), 0)
+            return bundle(d)
+        return bundle(d, 0, NX // 2) if way == 1 else bundle(d, NX // 2, NX)
+
+    def x2_send(step, way):
+        part = x2_part(step, way, way * (1 - step))
+        net.send(("x2", step, way), part, part, at_y(way))
+
+    seen = set()
+
+    def w_event(event):
+        kind, way = event[0], event[-1]
+        seen.add(event)
+        if kind == "y1":
+            step = event[1]
+            net.arrive(event, y1_part(step, way, -way * step), at_y(-way))
+            if step < ry:
+                y1_send(step + 1, way)
+        elif kind == "s2":
+            y2_send(event[1])
+        elif kind == "y2":
+            d = event[1]
+            part = w_y(c_at(d, -way))
+            net.arrive(event, part, at_x(-way))
+            if way == y3_way(d):
+                net.send(("y3", d), part, part, at_x(way))
+        elif kind == "y3":
+            d = event[1]
+            net.arrive(event, w_y(c_at(d, 2)), at_x(-y3_way(d)))
+        elif kind == "x1":
+            net.arrive(event, w_x(c_at(0, -way)), at_x(-way))
+            part = w_x(c_at(0, -way), x_lo if way == 1 else x_hi)
+            net.send(("x1r", way), part, part, at_x(way))
+        elif kind == "x1r":
+            net.arrive(event, w_x(c_at(0, 2), x_lo if way == 1 else x_hi), at_x(-way))
+            if ("x1r", -way) in seen:
+                x2_send(1, 1)
+                x2_send(1, -1)
+        elif kind == "x2":
+            step = event[1]
+            net.arrive(event, x2_part(step, way, -way * step), at_y(-way))
+            if step < ry:
+                x2_send(step + 1, way)
 
     def attend(h):
         lanes = slice(h * hs, (h + 1) * hs)
@@ -263,7 +290,7 @@
             here = col[h, rows, 0:1]
             pieces = []
             for j in range(i + 1):
-                gap = here - row[h : h + 1, j * strip : (j + 1) * strip]
+                gap = here - row[h][:, j * strip : (j + 1) * strip]
                 if j == i:
                     gap = jnp.where(t_in >= s_in, gap, -1e30)
                 pieces.append((scores[:, j * strip : (j + 1) * strip] * jnp.exp(gap)).astype(BF16))
@@ -272,7 +299,9 @@
 
     loads[2].wait()
     x1_send()
-    y1_send(1)
+    y1_send(1, 1)
+    y1_send(1, -1)
+    y2_send(0)
     loads[3].wait()
     attend(0)
 
@@ -294,11 +323,8 @@
     for d in sorted(range(1, ny), key=lambda d: -min(d, ny - d)):
         net.send(("p2", d), p2_send, p2_recv.at[d - 1], at_y(d), when=y + d < ny)
 
-    x1_relay()
-    y2_send(0)
-    y1_wait(1)
-    y2_send(1)
-    y2_send(-1)
+    for event in BEFORE_INCOMING:
+        w_event(event)
     attend(1)
 
     for d in range(1, ny):
@@ -318,10 +344,8 @@
     for d in (2, 1, 3):
         net.send(("p3", d), p3_send.at[xp(d)], p3_recv.at[x], at_x(d))
     p3_recv[pl.ds(x, 1)] = p3_send[pl.ds(x, 1)]
-    y1_send(2)
-    x1_wait()
-    x2_send(1)
-    y2_relay(0)
+    for event in BEFORE_MIXED:
+        w_event(event)
 
     for d in range(1, NX):
         net.arrive(("p3", d), p3_recv.at[xp(-d)], at_x(-d))
@@ -367,17 +391,6 @@
     hand(0, 0)
     hand(0, 1)
 
-    w_events = [
-        [lambda: y1_wait(2), lambda: y1_send(3), lambda: y2_send(2), lambda: y2_send(-2),
-         lambda: y2_relay(1), lambda: y2_relay(-1), lambda: x2_wait(1), lambda: x2_send(2)],
-        [lambda: y1_wait(3), lambda: y1_send(4), lambda: y2_send(3), lambda: y2_send(-3),
-         lambda: y2_relay(2), lambda: y2_relay(-2), lambda: x2_wait(2), lambda: x2_send(3)],
-        [lambda: y1_wait(4), lambda: y2_send(4), lambda: y2_relay(3), lambda: y2_relay(-3),
-         lambda: x2_wait(3), lambda: x2_send(4)],
-        [lambda: y2_relay(4)],
-        [lambda: x2_wait(4)] + [functools.partial(y3_wait, d) for d in (0, 1, -1, 2, -2, 3, -3, 4)],
-    ]
-
     def multiply(d, part, first=False):
         rows = pl.ds(part * half, half)
         base = zp(d)
@@ -392,30 +405,29 @@
             acc[rows, :] += result
 
     last = 2 * rz - 2
-    for i in range(last + 1):
-        for way in (1, -1):
-            z_wait(i, way)
-            if i + 2 <= last:
-                z_send(i + 2, way)
-            d, part = z_item(i, way)
-            hand(d - way, part)
-        if i < len(w_events):
-            for event in w_events[i]:
-                event()
-        if i == 4:
-            hand_wait(0, 0)
-            hand_wait(0, 1)
-            multiply(0, 0, True)
-            multiply(0, 1, True)
-            for d in (-1, 1, -2, 2):
-                for part in range(2):
-                    hand_wait(d, part)
-                    multiply(d, part)
-        if i == 5:
-            for d in (-3, 3):
-                for part in range(2):
-                    hand_wait(d, part)
-                    multiply(d, part)
+
+    def z_event(i, way):
+        z_wait(i, way)
+        if i + 2 <= last:
+            z_send(i + 2, way)
+        d, part = z_item(i, way)
+        hand(d - way, part)
+
+    for event in AFTER_MIXED:
+        if event[0] == "z":
+            z_event(*event[1:])
+        else:
+            w_event(event)
+    for d in (0, -1, 1, -2, 2):
+        for part in range(2):
+            hand_wait(d, part)
+            multiply(d, part, d == 0)
+    z_event(last, 1)
+    z_event(last, -1)
+    for d in (-3, 3):
+        for part in range(2):
+            hand_wait(d, part)
+            multiply(d, part)
     loads[4].wait()
     for part in range(2):
         rows = pl.ds(part * half, half)
@@ -448,7 +460,6 @@
             pltpu.VMEM((block, columns), BF16),
             pltpu.VMEM((block, width), BF16),
             pltpu.VMEM((block, columns), F32),
-            pltpu.VMEM((block, block), BF16),
             pltpu.VMEM((heads, block, hs), F32),
             pltpu.VMEM((heads, block, hs), F32),
             pltpu.VMEM((2 * nz, block, width), BF16),

time: 59.9 us -> 54.6 us (0.912)
  Pallas kernels: 59 us -> 53.7 us
    pallas_call x1, Pallas kernels: 59 us -> 53.7 us  [local(): pl.pallas_call(functools.partial(kernel, dims), out_shape=pltpu.VMEM((1,...]
where the time goes in v3:
time: 54.6 us; the launch traced here: 54.5 us
  Pallas kernels  53.7 us (98%)
  local copies, waits for them, and re-layouts  0.8 us (1%)
    pallas_call x1, Pallas kernels, local(): pl.pallas_call(functools.partial(kernel, dims), out_shape=pltpu.VMEM((1,...  53.7 us

profile of v3, /device:TPU:1, one launch (start us, length us, event | category | flops | bytes accessed | tf_op | source)
XLA Modules:
  0.0 54.5 jit_solution(10980660549066896561)
XLA Ops:
  0.0 53.7 %shard_map.82 = bf16[1,512,512]{2,1,0:T(8,128)(2,1)S(1)} custom-call(bf16[1,512,256]{2,1,0:T(8,128)(2,1)} %q_hbm.1, bf16[1,512,256]{2,1,0:T(8,128)(2,1)} %k_hbm.1, s32[1,512,256]{2,1,0:T(8,128)} %cnt_hbm.1, f32[1,256]{1,0:T(1,128)} %bitcast.2, f32[1,2,512]{2,1,0:T(2,128)} %ld_hbm.1, f32[1,256]{1,0:T(1,128)} %bitcast.3, bf16[128,512]{1,0:T(8,128)(2,1)} %w_hbm.1, ...), custom_call_target="tpu_custom_call" | custom-call | tf_op jit(solution)/shard_map/pallas_call | solution.py:448
  53.7 0.8 %copy.10 = bf16[1,512,512]{2,1,0:T(8,128)(2,1)} copy(bf16[1,512,512]{2,1,0:T(8,128)(2,1)S(1)} %shard_map.82) | data formatting | bytes 1048576

commit v4 on v3

--- a/solution.py
+++ b/solution.py
@@ -25,11 +25,16 @@
 )
 AFTER_MIXED = (
     ("y3", 0), ("y2", -2, -1), ("x2", 1, -1), ("x2", 1, 1), ("y3", 1), ("y2", 2, -1), ("y1", 3, -1), ("s2", 3),
-    ("y1", 3, 1), ("s2", -3), ("y2", -2, 1), ("y3", -1), ("z", 0, -1), ("z", 0, 1), ("y2", 2, 1), ("y3", -2),
-    ("x2", 2, -1), ("x2", 2, 1), ("z", 1, -1), ("z", 1, 1), ("y2", 3, 1), ("y1", 4, 1), ("y2", 3, -1), ("y1", 4, -1),
-    ("s2", 4), ("y2", -3, 1), ("y2", -3, -1), ("z", 2, -1), ("z", 2, 1), ("y3", 2), ("y2", 4, -1), ("y3", 3),
-    ("x2", 3, -1), ("z", 3, -1), ("z", 3, 1), ("x2", 3, 1), ("y3", -3), ("y2", 4, 1), ("y3", 4), ("z", 4, -1),
-    ("z", 4, 1), ("x2", 4, -1), ("x2", 4, 1), ("z", 5, -1), ("z", 5, 1),
+    ("y1", 3, 1), ("s2", -3), ("z", 0, -1), ("z", 0, 1), ("y2", -2, 1), ("y3", -1), ("z", 1, -1), ("z", 1, 1),
+    ("y2", 2, 1), ("y3", -2), ("z", 2, -1), ("z", 2, 1), ("x2", 2, -1), ("x2", 2, 1), ("y2", 3, 1), ("y1", 4, 1),
+    ("y2", 3, -1), ("y1", 4, -1), ("s2", 4), ("z", 3, -1), ("z", 3, 1), ("y2", -3, 1), ("y2", -3, -1), ("z", 4, -1),
+    ("z", 4, 1), ("z", 5, -1), ("z", 5, 1), ("y3", 2), ("y2", 4, -1), ("z", 6, -1), ("z", 6, 1), ("y3", 3),
+    ("x2", 3, -1), ("x2", 3, 1), ("y3", -3), ("z", 7, -1), ("z", 7, 1), ("y2", 4, 1), ("z", 8, -1), ("z", 8, 1),
+    ("y3", 4), ("z", 9, -1), ("z", 9, 1), ("x2", 4, -1), ("x2", 4, 1),
+)
+AFTER_WEIGHTS = (
+    ("z", 10, -1), ("z", 10, 1), ("z", 11, -1), ("z", 11, 1), ("z", 12, -1), ("z", 12, 1), ("z", 13, -1),
+    ("z", 13, 1),
 )
 
 
@@ -91,6 +96,7 @@
     half = block // 2
     ry, rz = ny // 2, nz // 2
     yr = wrows - xr
+    span = 2 * heads * hs // wrows
 
     def yp(d):
         return lax.rem(y + (d + ny), ny)
@@ -304,6 +310,7 @@
     y2_send(0)
     loads[3].wait()
     attend(0)
+    attend(1)
 
     for d in range(1, NX):
         net.arrive(("p1", d), p1_recv.at[xp(-d)], at_x(-d))
@@ -325,7 +332,6 @@
 
     for event in BEFORE_INCOMING:
         w_event(event)
-    attend(1)
 
     for d in range(1, ny):
         net.arrive(("p2", d), p2_recv.at[d - 1], at_y(-d), when=y >= d)
@@ -351,10 +357,10 @@
         net.arrive(("p3", d), p3_recv.at[xp(-d)], at_x(-d))
 
     def piece(t, part):
-        return a_all.at[t, pl.ds(part * half, half), :]
+        return a_all.at[t, pl.ds(part * strip, strip), :]
 
     def z_item(i, way):
-        return -way * (i // 2), (i % 2 if way == 1 else 1 - i % 2)
+        return -way * (i // 4), (i % 4 if way == 1 else (i + 2) % 4)
 
     def z_send(i, way):
         d, part = z_item(i, way)
@@ -377,64 +383,63 @@
         for h in range(heads)
     ]
     loads[7].wait()
-    for part in range(2):
-        rows = slice(part * half, (part + 1) * half)
+    for way, part in ((1, 0), (-1, 2), (1, 1), (-1, 3)):
+        rows = slice(part * strip, (part + 1) * strip)
         for h in range(heads):
             lanes = slice(h * hs, (h + 1) * hs)
             carried = jnp.dot(q[rows, lanes], incoming[h], preferred_element_type=F32)
             mixed = intra[h, rows, :] + jnp.exp(col[h, rows, :]) * carried
             scale = lax.rsqrt(jnp.mean(mixed * mixed, axis=1, keepdims=True) + EPSILON)
             a_all[ten, rows, lanes] = (mixed * scale * gain_ref[:, lanes]).astype(BF16)
-        z_send(part, 1)
-        z_send(1 - part, -1) if part else None
-    z_send(1, -1)
-    hand(0, 0)
-    hand(0, 1)
-
-    def multiply(d, part, first=False):
+        z_send(part % 2, way)
+    for i in (2, 3):
+        z_send(i, 1)
+        z_send(i, -1)
+    for part in range(4):
+        hand(0, part)
+
+    def multiply(d, part):
         rows = pl.ds(part * half, half)
+        for i in (2 * part, 2 * part + 1):
+            hand_wait(d, i)
         base = zp(d)
         result = None
         for c in range(2):
-            weight = w_all[pl.ds(base * 4 + 2 * c, 2)].reshape(2 * wrows, -1)
+            weight = w_all[pl.ds(base * span + c * (span // 2), span // 2)].reshape(span // 2 * wrows, -1)
             term = jnp.dot(a_all[base * 2 + c, rows, :], weight, preferred_element_type=F32)
             result = term if result is None else result + term
-        if first:
-            acc[rows, :] = result
-        else:
-            acc[rows, :] += result
-
-    last = 2 * rz - 2
+        return result
 
     def z_event(i, way):
         z_wait(i, way)
-        if i + 2 <= last:
-            z_send(i + 2, way)
+        if i + 4 < 4 * rz - 2:
+            z_send(i + 4, way)
         d, part = z_item(i, way)
         hand(d - way, part)
 
-    for event in AFTER_MIXED:
-        if event[0] == "z":
-            z_event(*event[1:])
-        else:
-            w_event(event)
+    def run(events):
+        for event in events:
+            if event[0] == "z":
+                z_event(*event[1:])
+            else:
+                w_event(event)
+
+    run(AFTER_MIXED)
+    halves = [pl.ds(part * half, half) for part in range(2)]
     for d in (0, -1, 1, -2, 2):
         for part in range(2):
-            hand_wait(d, part)
-            multiply(d, part, d == 0)
-    z_event(last, 1)
-    z_event(last, -1)
+            if d:
+                acc[halves[part], :] += multiply(d, part)
+            else:
+                acc[halves[part], :] = multiply(d, part)
+    run(AFTER_WEIGHTS)
     for d in (-3, 3):
         for part in range(2):
-            hand_wait(d, part)
-            multiply(d, part)
+            acc[halves[part], :] += multiply(d, part)
     loads[4].wait()
-    for part in range(2):
-        rows = pl.ds(part * half, half)
-        d = -4 if part == 0 else 4
-        hand_wait(d, part)
-        multiply(d, part)
-        out_ref[0, rows, :] = (res[rows, :].astype(F32) + acc[rows, :]).astype(BF16)
+    for part, d in ((0, -rz), (1, rz)):
+        total = acc[halves[part], :] + multiply(d, part)
+        out_ref[0, halves[part], :] = (res[halves[part], :].astype(F32) + total).astype(BF16)
     net.drain()
 
 
@@ -470,8 +475,8 @@
             pltpu.VMEM((ny - 1, depth, hs), BF16),
             pltpu.VMEM((NX, depth - 16, hs), BF16),
             pltpu.VMEM((NX, depth - 16, hs), BF16),
-            pltpu.SemaphoreType.DMA((96,)),
-            pltpu.SemaphoreType.DMA((96,)),
+            pltpu.SemaphoreType.DMA((120,)),
+            pltpu.SemaphoreType.DMA((120,)),
             pltpu.SemaphoreType.DMA((8,)),
         ],
         compiler_params=pltpu.CompilerParams(

time: 54.6 us -> 54.2 us (level)
  no operation moved by 1% of the time
where the time goes in v4:
time: 54.2 us; the launch traced here: 54.1 us
  Pallas kernels  53.3 us (98%)
  local copies, waits for them, and re-layouts  0.8 us (1%)
    pallas_call x1, Pallas kernels, local(): pl.pallas_call(functools.partial(kernel, dims), out_shape=pltpu.VMEM((1,...  53.3 us

profile of v4, /device:TPU:1, one launch (start us, length us, event | category | flops | bytes accessed | tf_op | source)
XLA Modules:
  0.0 54.1 jit_solution(1225015283013486768)
XLA Ops:
  0.0 53.3 %shard_map.82 = bf16[1,512,512]{2,1,0:T(8,128)(2,1)S(1)} custom-call(bf16[1,512,256]{2,1,0:T(8,128)(2,1)} %q_hbm.1, bf16[1,512,256]{2,1,0:T(8,128)(2,1)} %k_hbm.1, s32[1,512,256]{2,1,0:T(8,128)} %cnt_hbm.1, f32[1,256]{1,0:T(1,128)} %bitcast.2, f32[1,2,512]{2,1,0:T(2,128)} %ld_hbm.1, f32[1,256]{1,0:T(1,128)} %bitcast.3, bf16[128,512]{1,0:T(8,128)(2,1)} %w_hbm.1, ...), custom_call_target="tpu_custom_call" | custom-call | tf_op jit(solution)/shard_map/pallas_call | solution.py:453
  53.3 0.8 %copy.10 = bf16[1,512,512]{2,1,0:T(8,128)(2,1)} copy(bf16[1,512,512]{2,1,0:T(8,128)(2,1)S(1)} %shard_map.82) | data formatting | bytes 1048576

commit v5 on v4

--- a/solution.py
+++ b/solution.py
@@ -20,16 +20,16 @@
     ("x1", 1), ("x1", -1), ("y1", 1, 1), ("y1", 1, -1), ("s2", 1), ("s2", -1), ("x1r", 1), ("x1r", -1),
 )
 BEFORE_MIXED = (
-    ("y2", 0, -1), ("y2", 0, 1), ("y1", 2, 1), ("y1", 2, -1), ("y2", 1, 1), ("y2", 1, -1), ("s2", -2), ("s2", 2),
+    ("y2", 0, -1), ("y2", 0, 1), ("y1", 2, 1), ("y1", 2, -1), ("y2", 1, 1), ("s2", -2), ("s2", 2), ("y2", 1, -1),
     ("y2", -1, 1), ("y2", -1, -1),
 )
 AFTER_MIXED = (
     ("y3", 0), ("y2", -2, -1), ("x2", 1, -1), ("x2", 1, 1), ("y3", 1), ("y2", 2, -1), ("y1", 3, -1), ("s2", 3),
-    ("y1", 3, 1), ("s2", -3), ("z", 0, -1), ("z", 0, 1), ("y2", -2, 1), ("y3", -1), ("z", 1, -1), ("z", 1, 1),
-    ("y2", 2, 1), ("y3", -2), ("z", 2, -1), ("z", 2, 1), ("x2", 2, -1), ("x2", 2, 1), ("y2", 3, 1), ("y1", 4, 1),
-    ("y2", 3, -1), ("y1", 4, -1), ("s2", 4), ("z", 3, -1), ("z", 3, 1), ("y2", -3, 1), ("y2", -3, -1), ("z", 4, -1),
-    ("z", 4, 1), ("z", 5, -1), ("z", 5, 1), ("y3", 2), ("y2", 4, -1), ("z", 6, -1), ("z", 6, 1), ("y3", 3),
-    ("x2", 3, -1), ("x2", 3, 1), ("y3", -3), ("z", 7, -1), ("z", 7, 1), ("y2", 4, 1), ("z", 8, -1), ("z", 8, 1),
+    ("y1", 3, 1), ("s2", -3), ("y2", -2, 1), ("z", 0, -1), ("z", 0, 1), ("y3", -1), ("z", 1, -1), ("z", 1, 1),
+    ("y2", 2, 1), ("y3", -2), ("z", 2, -1), ("z", 2, 1), ("x2", 2, -1), ("x2", 2, 1), ("y2", 3, 1), ("y2", 3, -1),
+    ("y1", 4, 1), ("z", 3, -1), ("z", 3, 1), ("y1", 4, -1), ("s2", 4), ("y2", -3, 1), ("y2", -3, -1), ("z", 4, -1),
+    ("z", 4, 1), ("y3", 2), ("z", 5, -1), ("z", 5, 1), ("y2", 4, -1), ("z", 6, -1), ("z", 6, 1), ("y3", 3),
+    ("x2", 3, -1), ("x2", 3, 1), ("z", 7, -1), ("z", 7, 1), ("y3", -3), ("y2", 4, 1), ("z", 8, -1), ("z", 8, 1),
     ("y3", 4), ("z", 9, -1), ("z", 9, 1), ("x2", 4, -1), ("x2", 4, 1),
 )
 AFTER_WEIGHTS = (
@@ -311,6 +311,8 @@
     loads[3].wait()
     attend(0)
     attend(1)
+    for h in range(heads):
+        col[h] = jnp.exp(col[h])
 
     for d in range(1, NX):
         net.arrive(("p1", d), p1_recv.at[xp(-d)], at_x(-d))
@@ -388,7 +390,7 @@
         for h in range(heads):
             lanes = slice(h * hs, (h + 1) * hs)
             carried = jnp.dot(q[rows, lanes], incoming[h], preferred_element_type=F32)
-            mixed = intra[h, rows, :] + jnp.exp(col[h, rows, :]) * carried
+            mixed = intra[h, rows, :] + col[h, rows, :] * carried
             scale = lax.rsqrt(jnp.mean(mixed * mixed, axis=1, keepdims=True) + EPSILON)
             a_all[ten, rows, lanes] = (mixed * scale * gain_ref[:, lanes]).astype(BF16)
         z_send(part % 2, way)

time: 54.2 us -> 54.2 us (level)
  no operation moved by 1% of the time
where the time goes in v5:
time: 54.2 us; the launch traced here: 54.1 us
  Pallas kernels  53.3 us (98%)
  local copies, waits for them, and re-layouts  0.8 us (1%)
    pallas_call x1, Pallas kernels, local(): pl.pallas_call(functools.partial(kernel, dims), out_shape=pltpu.VMEM((1,...  53.3 us

profile of v5, /device:TPU:1, one launch (start us, length us, event | category | flops | bytes accessed | tf_op | source)
XLA Modules:
  0.0 54.1 jit_solution(14223058267007480064)
XLA Ops:
  0.0 53.3 %shard_map.82 = bf16[1,512,512]{2,1,0:T(8,128)(2,1)S(1)} custom-call(bf16[1,512,256]{2,1,0:T(8,128)(2,1)} %q_hbm.1, bf16[1,512,256]{2,1,0:T(8,128)(2,1)} %k_hbm.1, s32[1,512,256]{2,1,0:T(8,128)} %cnt_hbm.1, f32[1,256]{1,0:T(1,128)} %bitcast.2, f32[1,2,512]{2,1,0:T(2,128)} %ld_hbm.1, f32[1,256]{1,0:T(1,128)} %bitcast.3, bf16[128,512]{1,0:T(8,128)(2,1)} %w_hbm.1, ...), custom_call_target="tpu_custom_call" | custom-call | tf_op jit(solution)/shard_map/pallas_call | solution.py:455
  53.3 0.8 %copy.10 = bf16[1,512,512]{2,1,0:T(8,128)(2,1)} copy(bf16[1,512,512]{2,1,0:T(8,128)(2,1)S(1)} %shard_map.82) | data formatting | bytes 1048576
